TPU v7x, 128 devices: a whole 4x4x4 slice. The times are simulated.
128 devices in a mesh: seq: 8 (over x, core), head: 16 (over z, y).
Axes of the slice: x: 4, y: 4, z: 4, core: 2. Of those that a mesh axis runs over, the one named last changes fastest.
Arguments:
- moe_input: bfloat16 [16384, 1536], P(('seq', 'head')), may hold values from -6 to 6
- out_grad: bfloat16 [16384, 1536], P(('seq', 'head')), may hold values from -6 to 6
- route_ids: int32 [16384, 6], P(('seq', 'head')), may hold values from 0 to 63, all different within a row; in each aligned block of 128 rows (0 to 127, 128 to 255, ...) at most 16 rows name the same one
- route_gates: float32 [16384, 6], P(('seq', 'head')), may hold values from 0.05 to 0.35
- gate_halves: bfloat16 [128, 1536, 256], P(('seq', 'head')), may hold values from -0.15625 to 0.15625
- up_halves: bfloat16 [128, 1536, 256], P(('seq', 'head')), may hold values from -0.15625 to 0.15625
- down_halves: bfloat16 [128, 256, 1536], P(('seq', 'head')), may hold values from -0.25 to 0.25
- out_proj: bfloat16 [3072, 1536], P('head'), may hold values from -0.109375 to 0.109375
- ssd_x: float32 [16384, 3072], P('seq', 'head'), may hold values from -0.125 to 0.125
- b_proj: float32 [16384, 128], P('seq'), may hold values from -0.5 to 0.5
- c_proj: float32 [16384, 128], P('seq'), may hold values from -0.5 to 0.5
- log_decay: float32 [48, 16384], P('head', 'seq'), may hold values from -2.3 to 0, as said below
- skip_gain: float32 [48], P('head'), may hold values from 0.5 to 1.5
Outputs:
- resid_grad: bfloat16 [16384, 1536], P(('seq', 'head'))
- ssd_x_grad: float32 [16384, 3072], P('seq', 'head')
- b_grad: float32 [16384, 128], P(('seq', 'head'))
Inputs may be any that keep to these rules, and one draw needn't show every extreme that they name: `route_ids`: each row names 6 different experts; the 128 rows of one device name any one expert at most 16 times, a bound that some block reaches. `log_decay`: negative.
All inputs are finite; a program needn't handle non-finite values.
Results may differ from a plain program's by a relative error of at most 0.0039.
Values may be sent and summed in bfloat16 or wider, within the bound.
No kernel may reach another device: no remote copies, remote signals or barrier semaphores. Data moves between devices by JAX's collectives and lax.ppermute only.
A program may use at most 128 MiB of HBM per device.

v0:
```python
import jax
import jax.numpy as jnp
from jax import lax
from jax.sharding import PartitionSpec as P

BLOCK = 256


def entering(part, axis, combine, identity):
    count = lax.axis_size(axis)
    place = lax.axis_index(axis)
    ahead = count - 1 - place
    gathered = jax.tree.map(lambda a: lax.all_gather(a, axis), part)
    state = jax.tree.map(lambda a, e: jnp.zeros_like(a) + jnp.asarray(e, a.dtype), part, identity)

    def one(lap, state):
        source = count - 1 - lap
        return combine(
            state, jax.tree.map(lambda a: lax.dynamic_index_in_dim(a, source, 0, False), gathered)
        )

    return lax.fori_loop(0, ahead, one, state)


def swiglu_back(recv_input, recv_grad, gate_w, up_w, down_w):
    gate_act = jnp.einsum("shcd,hdf->shcf", recv_input, gate_w, preferred_element_type=jnp.float32)
    up_act = jnp.einsum("shcd,hdf->shcf", recv_input, up_w, preferred_element_type=jnp.float32)
    hidden_grad = jnp.einsum(
        "shcd,hfd->shcf", recv_grad, down_w, preferred_element_type=jnp.float32
    )
    sigmoid_act = jax.nn.sigmoid(gate_act)
    gate_grad = (
        hidden_grad * up_act * sigmoid_act * (1.0 + gate_act * (1.0 - sigmoid_act))
    ).astype(jnp.bfloat16)
    up_grad = (hidden_grad * gate_act * sigmoid_act).astype(jnp.bfloat16)
    result = jnp.einsum("shcf,hdf->shcd", gate_grad, gate_w, preferred_element_type=jnp.float32)
    return result + jnp.einsum("shcf,hdf->shcd", up_grad, up_w, preferred_element_type=jnp.float32)


def shards(
    moe_input,
    out_grad,
    route_ids,
    route_gates,
    gate_halves,
    up_halves,
    down_halves,
    out_proj,
    ssd_x,
    b_proj,
    c_proj,
    log_decay,
    skip_gain,
):
    highest = lax.Precision.HIGHEST
    tok_rows, feature_width = moe_input.shape
    top_count = route_ids.shape[1]
    devices = lax.axis_size(("seq", "head"))
    halves_dev = gate_halves.shape[0]
    experts = devices * halves_dev // 2
    capacity = tok_rows // 8
    flat_ids = route_ids.reshape(-1)
    onehot = (flat_ids[:, None] == jnp.arange(experts, dtype=jnp.int32)[None, :]).astype(jnp.int32)
    before = jnp.cumsum(onehot, axis=0) - onehot
    route_rank = jnp.sum(before * onehot, axis=1)
    route_slot = flat_ids * capacity + route_rank
    route_total = flat_ids.shape[0]
    filled = (
        jnp.zeros((experts * capacity,), jnp.int32)
        .at[route_slot]
        .set(jnp.arange(route_total, dtype=jnp.int32) + 1)
    )
    live_slot = filled > 0
    slot_token = jnp.maximum(filled - 1, 0) // top_count
    zero_row = jnp.zeros((), jnp.bfloat16)
    input_rows = jnp.where(live_slot[:, None], moe_input[slot_token], zero_row)
    grad_rows = jnp.where(live_slot[:, None], out_grad[slot_token], zero_row)

    def spread(rows):
        paired = jnp.broadcast_to(
            rows.reshape(experts, 1, capacity, feature_width), (experts, 2, capacity, feature_width)
        )
        return paired.reshape(devices, halves_dev, capacity, feature_width)

    recv_input = lax.all_to_all(
        spread(input_rows), ("seq", "head"), split_axis=0, concat_axis=0, tiled=True
    )
    recv_grad = lax.all_to_all(
        spread(grad_rows), ("seq", "head"), split_axis=0, concat_axis=0, tiled=True
    )
    half_terms = swiglu_back(recv_input, recv_grad, gate_halves, up_halves, down_halves)
    returned = lax.all_to_all(half_terms, ("seq", "head"), split_axis=0, concat_axis=0, tiled=True)
    expert_rows = (
        returned.reshape(experts, 2, capacity, feature_width).sum(axis=1).astype(jnp.bfloat16)
    )
    expert_rows = expert_rows.reshape(experts * capacity, feature_width)
    route_terms = expert_rows[route_slot].reshape(tok_rows, top_count, feature_width)
    moe_grad = jnp.sum(route_gates[:, :, None] * route_terms, axis=1)
    resid_grad = (out_grad.astype(jnp.float32) + moe_grad).astype(jnp.bfloat16)
    inner_dev = out_proj.shape[0]
    heads_dev = skip_gain.shape[0]
    head_dim = inner_dev // heads_dev
    seq_rows, state_dim = b_proj.shape
    block_len = BLOCK
    block_count = seq_rows // block_len
    decay = log_decay.reshape(heads_dev, block_count, block_len)
    within = jnp.cumsum(decay, axis=2)
    block_sum = within[:, :, -1]
    offset = jnp.cumsum(block_sum, axis=1) - block_sum
    total = offset[:, -1] + block_sum[:, -1]
    b_blocks = b_proj.reshape(block_count, block_len, state_dim)
    c_blocks = c_proj.reshape(block_count, block_len, state_dim)
    x_blocks = ssd_x.reshape(block_count, block_len, heads_dev, head_dim)
    scores = jnp.einsum("btn,bsn->bts", c_blocks, b_blocks, precision=highest)
    causal = jnp.arange(block_len)[:, None] >= jnp.arange(block_len)[None, :]
    log_gap = within[:, :, :, None] - within[:, :, None, :]
    weights = jnp.where(causal, jnp.exp(jnp.where(causal, log_gap, 0.0)), 0.0) * scores[None]
    to_start = jnp.exp(within)
    to_end = jnp.exp(block_sum[:, :, None] - within)
    block_decay = jnp.exp(block_sum)
    ssd_grad = jnp.einsum(
        "td,kd->tk",
        lax.all_gather(resid_grad, "head", axis=0, tiled=True),
        out_proj,
        preferred_element_type=jnp.float32,
    )
    g_blocks = ssd_grad.reshape(block_count, block_len, heads_dev, head_dim)
    intra_x = jnp.einsum("hbts,bthp->bshp", weights, g_blocks, precision=highest)
    inner_prod = jnp.einsum("bthp,bshp->hbts", g_blocks, x_blocks, precision=highest)
    intra_b = jnp.einsum("hbts,btn->bsn", weights * inner_prod, c_blocks, precision=highest)
    block_state = jnp.einsum("hbt,bthp,btn->bhpn", to_start, g_blocks, c_blocks, precision=highest)

    def block_step(carry, blocks_in):
        factor, summary = blocks_in
        return (factor[:, None, None] * carry + summary, carry)

    zero_state = jnp.zeros((heads_dev, head_dim, state_dim), jnp.float32)
    dev_state, future_local = lax.scan(
        block_step, zero_state, (block_decay.T, block_state), reverse=True
    )
    dev_decay = jnp.exp(total)

    def combine_pair(earlier, later):
        return (earlier[0] * later[0], later[0][:, None, None] * earlier[1] + later[1])

    identity = (jnp.ones((heads_dev,), jnp.float32), zero_state)
    incoming = entering((dev_decay, dev_state), "seq", combine_pair, identity)[1]
    tail_block = jnp.exp(total[:, None] - offset - block_sum)
    future = future_local + tail_block.T[:, :, None, None] * incoming[None]
    cross_x = jnp.einsum("hbs,bsn,bhpn->bshp", to_end, b_blocks, future, precision=highest)
    grad_x = intra_x + cross_x + skip_gain[None, None, :, None] * g_blocks
    cross_b = jnp.einsum("hbs,bshp,bhpn->bsn", to_end, x_blocks, future, precision=highest)
    partial_b = (intra_b + cross_b).reshape(seq_rows, state_dim)
    b_grad = lax.psum_scatter(partial_b, "head", scatter_dimension=0, tiled=True)
    return (resid_grad, grad_x.reshape(seq_rows, inner_dev), b_grad)


def solution(mesh):
    return jax.shard_map(
        shards,
        mesh=mesh,
        in_specs=(
            P(("seq", "head"), None),
            P(("seq", "head"), None),
            P(("seq", "head"), None),
            P(("seq", "head"), None),
            P(("seq", "head"), None, None),
            P(("seq", "head"), None, None),
            P(("seq", "head"), None, None),
            P("head", None),
            P("seq", "head"),
            P("seq", None),
            P("seq", None),
            P("head", "seq"),
            P("head"),
        ),
        out_specs=(P(("seq", "head"), None), P("seq", "head"), P(("seq", "head"), None)),
        check_vma=False,
    )
```

profile of v0, /device:TPU:0, one launch (start us, length us, event | category | flops | bytes accessed | tf_op | source)
XLA Modules:
  0.0 659.2 jit_solution(17061906879405171368)
XLA Ops:
  11.6 3.4 scatter_custom_fusion
  15.1 5.6 gather_fusion.1
  20.6 5.6 gather_fusion
  26.3 3.1 broadcast_select_fusion.1
  30.3 86.4 %all_to_all.15 = bf16[128,1,16,1536]{3,2,1,0:T(8,128)(2,1)} all-to-all(bf16[128,1,16,1536]{3,2,1,0:T(8,128)(2,1)S(1)} %bitcast.218), channel_id=1, replica_groups=mesh['seq'=8,'head'=16] {'seq','head'}, dimensions={0} | all-to-all | bytes 12582912 | tf_op jit(solution)/shard_map/all_to_all | solution.py:85
  116.6 3.5 broadcast_in_dim.82
  120.1 6.3 all-to-all-start
  126.5 10.0 %fusion.1 = f32[128,16,256]{2,0,1:T(8,128)S(1)} fusion(bf16[128,1,16,1536]{3,2,1,0:T(8,128)(2,1)} %all_to_all.15, bf16[1,1536,256]{2,1,0:T(8,128)(2,1)} %param.21), kind=kOutput, calls=%fused_computation.13 | convolution fusion | flops 1610612736 | bytes 9175040 | tf_op jit(solution)/shard_map/shcd,hdf->shcf/dot_general | solution.py:26
  136.5 69.1 %all-to-all-done = bf16[128,1,16,1536]{3,2,1,0:T(8,128)(2,1)} async-done(((bf16[128,1,16,1536]{3,2,1,0:T(8,128)(2,1)}), bf16[128,1,16,1536]{3,2,1,0:T(8,128)(2,1)}, u32[]{:S(2)}, u32[]{:S(2)}) %all-to-all-start) | async-done | bytes 6291488 | tf_op jit(solution)/shard_map/all_to_all | solution.py:88
  205.6 11.6 %fusion.5 = f32[128,16,256]{2,0,1:T(8,128)} fusion(bf16[128,1,16,1536]{3,2,1,0:T(8,128)(2,1)} %all-to-all-done, bf16[1,256,1536]{2,1,0:T(8,128)(2,1)} %param.23), kind=kOutput, calls=%fused_computation.17 | convolution fusion | flops 1610612736 | bytes 9175040 | tf_op jit(solution)/shard_map/shcd,hfd->shcf/dot_general | solution.py:28
  217.1 19.3 %fusion.45 = f32[128,16,1536]{2,0,1:T(8,128)} fusion(f32[128,16,256]{2,0,1:T(8,128)S(1)} %fusion.1, bf16[128,1,16,1536]{3,2,1,0:T(8,128)(2,1)} %all_to_all.15, f32[128,16,256]{2,0,1:T(8,128)} %fusion.5, bf16[1,1536,256]{2,1,0:T(8,128)(2,1)} %param.21, bf16[1,1536,256]{2,1,0:T(8,128)(2,1)} %param.22), kind=kOutput, calls=%fused_computation.60 | convolution fusion | flops 3226468352 | bytes 24641536 | tf_op jit(solution)/shard_map/shcf,hdf->shcd/dot_general | solution.py:36
  236.4 11.8 %add_bitcast_fusion = f32[128,1,16,1536]{3,0,2,1:T(8,128)} fusion(f32[128,16,1536]{2,0,1:T(8,128)} %fusion.45, f32[128,16,256]{2,0,1:T(8,128)} %fusion.5, f32[128,16,256]{2,0,1:T(8,128)S(1)} %fusion.1, bf16[1,1536,256]{2,1,0:T(8,128)(2,1)} %param.22), kind=kOutput, calls=%fused_computation.11 | convolution fusion | flops 1616904192 | bytes 30146560 | tf_op jit(solution)/shard_map/shcf,hdf->shcd/dot_general | solution.py:37
  248.3 16.4 %copy.76 = f32[128,1,16,1536]{3,2,1,0:T(8,128)} copy(f32[128,1,16,1536]{3,0,2,1:T(8,128)} %add_bitcast_fusion) | data formatting | bytes 25165824 | tf_op jit(solution)/shard_map/add | solution.py:37
  264.7 6.1 all-to-all-start.2
  271.3 161.2 %all-to-all-done.2 = f32[128,1,16,1536]{3,2,1,0:T(8,128)} async-done(((f32[128,1,16,1536]{3,2,1,0:T(8,128)}), f32[128,1,16,1536]{3,2,1,0:T(8,128)}, u32[]{:S(2)}, u32[]{:S(2)}) %all-to-all-start.2) | async-done | bytes 12582944 | tf_op jit(solution)/shard_map/all_to_all | solution.py:92
  432.5 6.4 bitcast_reduce_fusion
  440.7 3.4 copy.78
  444.1 8.2 %gather_fusion.2 = bf16[768,1536]{1,0:T(8,128)(2,1)} fusion(bf16[1024,1536]{1,0:T(8,128)(2,1)} %bitcast.216, s32[1024]{0:T(1024)S(1)} %pad_clamp_fusion), kind=kCustom, calls=%fused_computation.2 | custom fusion | bytes 4721664 | tf_op jit(solution)/shard_map/gather | solution.py:97
  452.3 5.0 reshape.227
  457.3 5.2 multiply_reduce_fusion.1
  468.3 13.8 %all-reduce = f32[24]{0:T(128)S(1)} all-reduce(f32[24]{0:T(128)S(1)} %dynamic-update-slice), channel_id=2, replica_groups=mesh['seq'=8,'head'=16] {'seq'}, use_global_device_ids=true, to_apply=%add | all-reduce | flops 24 | bytes 192
  485.2 4.5 fusion.77
  489.6 33.6 %all-gather.4.cloned.1.call-done = bf16[2048,1536]{1,0:T(8,128)(2,1)} async-done(((bf16[128,1536]{1,0:T(8,128)(2,1)}), bf16[2048,1536]{1,0:T(8,128)(2,1)}) %all-gather.4.cloned.1.call-update) | async-done | bytes 6291472 | tf_op jit(solution)/shard_map/all_gather | solution.py:123
  523.2 5.0 fusion.76
  531.8 8.3 %while.32 = (s32[]{:T(128)}, f32[3,64,128]{2,1,0:T(8,128)S(1)}, f32[8,3,64,128]{3,2,1,0:T(8,128)S(1)}, f32[8,3]{1,0:T(8,128)S(1)}, f32[8,3,64,128]{3,2,1,0:T(8,128)}, /*index=5*/s32[]{:T(128)}, s32[]{:T(128)}, s32[]{:T(128)}) while((s32[]{:T(128)}, f32[3,64,128]{2,1,0:T(8,128)S(1)}, f32[8,3,64,128]{3,2,1,0:T(8,128)S(1)}, ...), condition=%wide.region_9.10_spmd.clone, body=%wide.region_8.9_spmd.clone.sunk | while | flops 98308 | bytes 491676 | solution.py:138
  540.1 14.8 %all-gather.1 = f32[24,64,128]{2,1,0:T(8,128)} all-gather(f32[3,64,128]{2,1,0:T(8,128)S(1)} %get-tuple-element.192), channel_id=3, replica_groups=mesh['seq'=8,'head'=16] {'seq'}, dimensions={0}, use_global_device_ids=true | all-gather | bytes 884736 | tf_op jit(solution)/shard_map/all_gather | solution.py:13
  554.9 7.2 %while.31 = (s32[]{:T(128)}, f32[3,64,128]{2,1,0:T(8,128)S(1)}, s32[]{:T(128)}, f32[8,3]{1,0:T(8,128)S(1)}, f32[8,3,64,128]{3,2,1,0:T(8,128)}, /*index=5*/s32[]{:T(128)}, s32[]{:T(128)}, s32[]{:T(128)}, s32[]{:T(128)}) while((s32[]{:T(128)}, f32[3,64,128]{2,1,0:T(8,128)S(1)}, s32[]{:T(128)}, f32[8,3]{1,0:T(8,128)S(1)}, ...), condition=%wide.region_12.13_spmd, body=%wide.region_11.12_spmd.sunk | while | flops 49158 | bytes 295095 | solution.py:22
  562.0 10.2 %multiply_reduce_fusion = f32[8,256,256]{2,1,0:T(8,128)S(1)} fusion(f32[8,256,256]{2,1,0:T(8,128)} %fusion.77, f32[3,8,256]{2,0,1:T(4,128)} %copy.80, pred[256,256]{1,0:T(8,128)(4,1)} %iota_compare_fusion, f32[8,256,3,64]{1,0,3,2:T(8,128)S(1)} %bitcast.221, f32[8,256,3,64]{1,0,3,2:T(8,128)} %bitcast.225), kind=kOutput, calls=%fused_computation.20 | convolution fusion | flops 1216872448 | bytes 7430144 | tf_op jit(solution)/shard_map/bthp,bshp->hbts/dot_general | solution.py:129
  572.2 3.9 fusion.38
  576.1 4.5 convolution_add_fusion
  583.6 6.2 fusion.28
  592.5 59.6 %reduce-scatter.2.cloned.1.call-done = f32[128,128]{1,0:T(8,128)} async-done(((f32[2048,128]{1,0:T(8,128)}), f32[128,128]{1,0:T(8,128)}) %reduce-scatter.2.cloned.1.call-update) | async-done | bytes 65552 | tf_op jit(solution)/shard_map/reduce_scatter | solution.py:154
  (121 shorter events, 39.8 us)
Async XLA Ops:
  7.2 478.0 %copy-start = (f32[2048,128]{1,0:T(8,128)S(1)}, f32[2048,128]{1,0:T(8,128)}, u32[]{:S(2)}) copy-start(f32[2048,128]{1,0:T(8,128)} %param.27) | copy-start | bytes 3145732
  7.2 7.9 %copy-start.2 = (bf16[128,1536]{1,0:T(8,128)(2,1)S(1)}, bf16[128,1536]{1,0:T(8,128)(2,1)}, u32[]{:S(2)}) copy-start(bf16[128,1536]{1,0:T(8,128)(2,1)} %param.17) | copy-start | bytes 1179652
  15.0 5.6 copy-start.1
  120.1 85.5 %all-to-all-start = ((bf16[128,1,16,1536]{3,2,1,0:T(8,128)(2,1)}), bf16[128,1,16,1536]{3,2,1,0:T(8,128)(2,1)}, u32[]{:S(2)}, u32[]{:S(2)}) async-start(bf16[128,1,16,1536]{3,2,1,0:T(8,128)(2,1)} %bitcast.217), calls=%async_computation | async-start | bytes 12582912 | tf_op jit(solution)/shard_map/all_to_all | solution.py:88
  264.7 6.5 copy-start.9
  264.7 167.8 %all-to-all-start.2 = ((f32[128,1,16,1536]{3,2,1,0:T(8,128)}), f32[128,1,16,1536]{3,2,1,0:T(8,128)}, u32[]{:S(2)}, u32[]{:S(2)}) async-start(f32[128,1,16,1536]{3,2,1,0:T(8,128)} %copy.76), calls=%async_computation.2 | async-start | bytes 25165824 | tf_op jit(solution)/shard_map/all_to_all | solution.py:92
  270.8 252.5 %all-gather.4.cloned.1.call-start = ((), (), s32[]{:S(2)}) async-start(), calls=%async_computation.4 | async-start | bytes 6684672 | tf_op jit(solution)/shard_map/all_gather | solution.py:123
  457.3 6.1 copy-start.7
  462.5 4.4 copy-start.12
  463.3 188.8 %reduce-scatter.2.cloned.1.call-start = ((), (), s32[]{:S(2)}) async-start(), calls=%async_computation.5 | async-start | bytes 1114112 | tf_op jit(solution)/shard_map/reduce_scatter | solution.py:154
  485.2 38.0 %copy-start.10 = (bf16[192,1536]{1,0:T(8,128)(2,1)S(1)}, bf16[192,1536]{1,0:T(8,128)(2,1)}, u32[]{:S(2)}) copy-start(bf16[192,1536]{1,0:T(8,128)(2,1)} %param.24) | copy-start | bytes 1769476
  528.8 3.0 copy-start.3
  580.6 2.9 copy-start.4
  580.6 3.0 copy-start.11
  580.6 2.9 copy-start.5
  580.7 2.9 copy-start.6
  580.7 2.9 copy-start.8
Sparse Core Ops, SparseCore 0:
  463.5 59.7 all-gather.3
  580.8 71.3 reduce-scatter.1
where the time goes:
time: 665 us; the launch traced here: 659 us
  waiting for transfers between devices  323 us (49%)
  blocking collectives  115 us (17%)
  matrix products  92.7 us (14%)
  local copies, waits for them, and re-layouts  63.2 us (10%)
  other arithmetic  36.2 us (5%)
  between operations  15.3 us (2%)
  starting transfers between devices  12.9 us (2%)
    all_to_all x1, waiting for transfers between devices, shards(): lax.all_to_all(half_terms, ('seq', 'head'), split_axis=0, concat_axis=0,...  161 us
    all_to_all x1, blocking collectives, shards(): lax.all_to_all(spread(input_rows), ('seq', 'head'), split_axis=0, concat_...  86.4 us
    all_to_all x1, waiting for transfers between devices, shards(): lax.all_to_all(spread(grad_rows), ('seq', 'head'), split_axis=0, concat_a...  69.1 us
    reduce_scatter x1, waiting for transfers between devices, shards(): lax.psum_scatter(partial_b, 'head', scatter_dimension=0, tiled=True)  59.6 us
    all_gather x1, waiting for transfers between devices, shards(): lax.all_gather(resid_grad, 'head', axis=0, tiled=True)  33.6 us
    dot_general x1, matrix products, swiglu_back(): jnp.einsum('shcf,hdf->shcd', gate_grad, gate_w, preferred_element_type=jn...  19.3 us
    add x1, local copies, waits for them, and re-layouts, swiglu_back(): result + jnp.einsum('shcf,hdf->shcd', up_grad, up_w, preferred_element_ty...  16.4 us
    all_gather x1, blocking collectives, entering(): gathered = jax.tree.map(lambda a: lax.all_gather(a, axis), part)  14.8 us
  transfers between devices with their start and end apart: 4, of which 4 were waited for; matrix products, arithmetic and copies ran while one was open for 5% of the time, Pallas kernels for 0%

commit v1 on v0

v1 whole, which is shorter than its diff:
```python
import functools

import jax
import jax.numpy as jnp
from jax import lax
from jax.experimental import pallas as pl
from jax.experimental.pallas import tpu as pltpu
from jax.sharding import PartitionSpec as P

BLOCK = 256
SLOTS = 8
F32 = jnp.float32
BF16 = jnp.bfloat16
HIGHEST = lax.Precision.HIGHEST
NT = (((1,), (1,)), ((), ()))
NN = (((1,), (0,)), ((), ()))
TN = (((0,), (0,)), ((), ()))


def params(mib=48):
    return pltpu.CompilerParams(vmem_limit_bytes=mib << 20)


def cost(flops, bytes_accessed):
    return pl.CostEstimate(flops=int(flops), bytes_accessed=int(bytes_accessed), transcendentals=0)


def split(a):
    hi = a.astype(BF16)
    return hi, (a - hi.astype(F32)).astype(BF16)


def dot(a, b, dims):
    return lax.dot_general(a, b, dims, preferred_element_type=F32)


def dot_high(a, b, dims):
    return lax.dot_general(a, b, dims, precision=HIGHEST, preferred_element_type=F32)


def slot_experts(rows, toks):
    row = lax.broadcasted_iota(jnp.int32, (rows, toks), 0)
    dev, slot = row >> 3, row & 7
    x, core, z, y = dev >> 5, (dev >> 4) & 1, (dev >> 2) & 3, dev & 3
    expert = (2 * x + (y & 1)) * 8 + 2 * z + (y >> 1)
    return expert, 2 * slot + core


def select_kernel(ids_ref, rows_ref, sel_ref, out_ref):
    slots, toks = sel_ref.shape
    expert, rank = slot_experts(slots, toks)
    named = ids_ref[0:1, :] == expert
    for k in range(1, ids_ref.shape[0]):
        named = jnp.logical_or(named, ids_ref[k : k + 1, :] == expert)
    named = jnp.where(named, 1.0, 0.0)
    earlier = jnp.where(
        lax.broadcasted_iota(jnp.int32, (toks, toks), 0)
        < lax.broadcasted_iota(jnp.int32, (toks, toks), 1),
        1.0,
        0.0,
    )
    before = dot(named.astype(BF16), earlier.astype(BF16), NN)
    sel = jnp.where(before == rank.astype(F32), named, 0.0).astype(BF16)
    sel_ref[...] = sel
    out_ref[...] = dot(sel, rows_ref[...], NN).astype(BF16)


def second_kernel(ids_ref, gates_ref, sel_ref, rows_ref, out_ref, hi_ref, lo_ref):
    slots, toks = sel_ref.shape
    out_ref[...] = dot(sel_ref[...], rows_ref[...], NN).astype(BF16)
    expert, _ = slot_experts(slots, toks)
    gate = jnp.zeros((slots, toks), F32)
    for k in range(ids_ref.shape[0]):
        gate = jnp.where(ids_ref[k : k + 1, :] == expert, gates_ref[k : k + 1, :], gate)
    mix = (gate * sel_ref[...].astype(F32)).T
    hi, lo = split(mix)
    hi_ref[...] = hi
    lo_ref[...] = lo


def combine_kernel(hi_ref, lo_ref, rows_ref, grad_ref, out_ref):
    rows = rows_ref[...]
    total = dot(hi_ref[...], rows, NN) + dot(lo_ref[...], rows, NN)
    out_ref[...] = (grad_ref[...].astype(F32) + total).astype(BF16)


def load_weights(home, own, far, bufs, sem):
    def copies(sources):
        return [pltpu.make_async_copy(s, b, sem.at[i]) for i, (s, b) in enumerate(zip(sources, bufs))]

    @pl.when(pl.program_id(0) == 0)
    def _():
        @pl.when(home == 1)
        def _():
            for c in copies(own):
                c.start()

        @pl.when(home == 0)
        def _():
            for c in copies(far):
                c.start()

        for c in copies(own):
            c.wait()


def acts_kernel(home_ref, x_ref, *refs):
    own, far, (gate_ref, up_ref), bufs, sem = refs[:4], refs[4:8], refs[8:10], refs[10:14], refs[14]
    load_weights(home_ref[0], own, far, bufs, sem)
    x = x_ref[...]
    half = bufs[0].shape[2]
    for j in range(2):
        gate_ref[:, j * half : (j + 1) * half] = dot(x, bufs[j][0], NN)
        up_ref[:, j * half : (j + 1) * half] = dot(x, bufs[2 + j][0], NN)


def back_kernel(home_ref, g_ref, gate_ref, up_ref, *refs):
    own, far, out_ref, bufs, sem = refs[:6], refs[6:12], refs[12], refs[13:19], refs[19]
    load_weights(home_ref[0], own, far, bufs, sem)
    g = g_ref[...]
    half = bufs[0].shape[2]
    total = None
    for j in range(2):
        hidden = dot(g, bufs[4 + j][0], NT)
        gate_act = gate_ref[:, j * half : (j + 1) * half]
        up_act = up_ref[:, j * half : (j + 1) * half]
        sig = jax.nn.sigmoid(gate_act)
        gate_grad = (hidden * up_act * sig * (1.0 + gate_act * (1.0 - sig))).astype(BF16)
        up_grad = (hidden * gate_act * sig).astype(BF16)
        part = dot(gate_grad, bufs[j][0], NT) + dot(up_grad, bufs[2 + j][0], NT)
        total = part if total is None else total + part
    out_ref[...] = total.astype(BF16)


def prepare_kernel(d_ref, b_ref, c_ref, x_ref, w_ref, ts_ref, te_ref, xte_ref, bs_ref, tail_ref, tot_ref):
    heads, n = d_ref.shape
    dim = x_ref.shape[1] // heads
    row = lax.broadcasted_iota(jnp.int32, (n, n), 0)
    col = lax.broadcasted_iota(jnp.int32, (n, n), 1)
    tri = jnp.where(col <= row, 1.0, 0.0)
    spread = jnp.concatenate(
        [jnp.broadcast_to(d_ref[h : h + 1, :], (dim, n)) for h in range(heads)], axis=0
    )
    across = dot_high(spread, tri, NT)
    down = dot_high(tri, spread, NT)
    scores = dot_high(b_ref[...], c_ref[...], NT)
    later = col >= row
    for h in range(heads):
        gap = across[h * dim : h * dim + 1, :] - down[:, h * dim : h * dim + 1]
        w = jnp.where(later, jnp.exp(jnp.where(later, gap, 0.0)), 0.0) * scores
        w_ref[0, h] = w.astype(BF16)
    ts_ref[...] = jnp.exp(down)
    te = jnp.exp(down[n - 1 : n, :] - down)
    te_ref[...] = te
    xte_ref[...] = (x_ref[...] * te).astype(BF16)

    @pl.when(pl.program_id(0) == 0)
    def _():
        tot_ref[...] = jnp.zeros_like(tot_ref)

    block_sum = jnp.broadcast_to(across[:, n - 1 : n], tot_ref.shape)
    bs_ref[0] = block_sum
    tail_ref[0] = tot_ref[...]
    tot_ref[...] = tot_ref[...] + block_sum


def grad_kernel(r_ref, p_ref, c_ref, ts_ref, bs_ref, tot_ref, g_ref, fut_ref, pay_ref, carry_ref):
    @pl.when(pl.program_id(0) == 0)
    def _():
        carry_ref[...] = jnp.zeros_like(carry_ref)

    g = dot(r_ref[...], p_ref[...], NT)
    g_ref[...] = g
    ghi, glo = split(g * ts_ref[...])
    chi, clo = split(c_ref[...])
    state = dot(ghi, chi, TN) + dot(ghi, clo, TN) + dot(glo, chi, TN)
    carry = carry_ref[...]
    fut_ref[0] = carry
    carry = jnp.exp(bs_ref[0]) * carry + state
    carry_ref[...] = carry
    rows, lanes = carry.shape
    heads = 3
    dim = rows // heads
    pay_ref[0:rows, :] = carry
    pay_ref[rows:, :] = jnp.concatenate(
        [tot_ref[h * dim : h * dim + 1, :] for h in range(heads)]
        + [jnp.zeros((pay_ref.shape[0] - rows - heads, lanes), F32)],
        axis=0,
    )


def intra_kernel(w_ref, g_ref, x_ref, c_ref, skip_ref, gx_ref, ib_ref):
    heads = w_ref.shape[1]
    dim = g_ref.shape[1] // heads
    acc = None
    for h in range(heads):
        w = w_ref[0, h]
        cols = slice(h * dim, (h + 1) * dim)
        g = g_ref[:, cols]
        gb = g.astype(BF16)
        gx_ref[:, cols] = dot(w, gb, NN) + skip_ref[:, cols] * g
        inner = dot(x_ref[:, cols].astype(BF16), gb, NT)
        term = w.astype(F32) * inner
        acc = term if acc is None else acc + term
    ib_ref[...] = dot(acc.astype(BF16), c_ref[...].astype(BF16), NN)


def cross_b_kernel(*refs):
    pays, (fut_ref, tail_ref, xte_ref, ib_ref, pb_ref, all_ref, in_ref) = refs[:-7], refs[-7:]
    rows, lanes = in_ref.shape
    heads = 3
    dim = rows // heads

    @pl.when(pl.program_id(0) == 0)
    def _():
        acc = pays[0][0:rows, :]
        log = jnp.zeros((rows, lanes), F32)
        for prev, cur in zip(pays[:-1], pays[1:]):
            log = log + jnp.concatenate(
                [jnp.broadcast_to(prev[rows + h : rows + h + 1, :], (dim, lanes)) for h in range(heads)],
                axis=0,
            )
            acc = acc + jnp.exp(log) * cur[0:rows, :]
        in_ref[...] = acc

    future = fut_ref[0] + jnp.exp(tail_ref[0]) * in_ref[...]
    hi, lo = split(future)
    all_ref[0] = hi
    xte = xte_ref[...]
    pb_ref[...] = ib_ref[...] + dot(xte, hi, NN) + dot(xte, lo, NN)


def cross_x_kernel(all_ref, te_ref, b_ref, gx_ref, out_ref):
    bhi, blo = split(b_ref[...])
    fut = all_ref[0]
    out_ref[...] = gx_ref[...] + te_ref[...] * (dot(bhi, fut, NT) + dot(blo, fut, NT))


def whole(shape):
    zeros = (0,) * len(shape)
    return pl.BlockSpec(shape, lambda *_: zeros)


def shards(
    moe_input,
    out_grad,
    route_ids,
    route_gates,
    gate_halves,
    up_halves,
    down_halves,
    out_proj,
    ssd_x,
    b_proj,
    c_proj,
    log_decay,
    skip_gain,
):
    sds = jax.ShapeDtypeStruct
    toks, width = moe_input.shape
    n_seq, n_head = lax.axis_size("seq"), lax.axis_size("head")
    devices = n_seq * n_head
    slots = devices * SLOTS
    both = ("seq", "head")
    any_spec = pl.BlockSpec(memory_space=pl.ANY)
    smem_spec = pl.BlockSpec(memory_space=pltpu.SMEM)

    seq, head = lax.axis_index("seq"), lax.axis_index("head")
    home = ((seq & 1) == (head & 1)).astype(jnp.int32).reshape(1)
    over_y, over_core = [], []
    for s in range(n_seq):
        for h in range(n_head):
            if (s & 1) != (h & 1):
                over_y.append((s * n_head + h, s * n_head + (h ^ 1)))
            else:
                over_core.append((s * n_head + h, (s ^ 1) * n_head + h))
    halves = (gate_halves, up_halves, down_halves)
    y_halves = [lax.ppermute(a, both, over_y) for a in halves]
    far_own = [lax.ppermute(a, both, over_core) for a in halves]
    far_y = [lax.ppermute(a, both, over_core) for a in y_halves]

    ids_t, gates_t = route_ids.T, route_gates.T
    sel, send_input = pl.pallas_call(
        select_kernel,
        out_shape=(sds((slots, toks), BF16), sds((slots, width), BF16)),
        compiler_params=params(),
        cost_estimate=cost(2 * slots * toks * width, 4 << 20),
        name="select_rows",
    )(ids_t, moe_input)
    send_grad, mix_hi, mix_lo = pl.pallas_call(
        second_kernel,
        out_shape=(sds((slots, width), BF16), sds((toks, slots), BF16), sds((toks, slots), BF16)),
        compiler_params=params(),
        cost_estimate=cost(2 * slots * toks * width, 4 << 20),
        name="select_grads",
    )(ids_t, gates_t, sel, out_grad)

    def exchange(rows):
        shaped = rows.reshape(devices, SLOTS, width)
        return lax.all_to_all(shaped, both, split_axis=0, concat_axis=0, tiled=True).reshape(slots, width)

    recv_input = exchange(send_input)
    recv_grad = exchange(send_grad)

    tile = 256
    half = gate_halves.shape[2]
    hidden = 2 * half
    row_spec = pl.BlockSpec((tile, width), lambda i: (i, 0))
    act_spec = pl.BlockSpec((tile, hidden), lambda i: (i, 0))
    in_buf = pltpu.VMEM((1, width, half), BF16)
    out_buf = pltpu.VMEM((1, half, width), BF16)
    own = [a for o, y in zip(halves, y_halves) for a in (o, y)]
    far = [a for o, y in zip(far_own, far_y) for a in (o, y)]
    gate_act, up_act = pl.pallas_call(
        acts_kernel,
        grid=(slots // tile,),
        in_specs=[smem_spec, row_spec] + [any_spec] * 8,
        out_specs=(act_spec, act_spec),
        out_shape=(sds((slots, hidden), F32), sds((slots, hidden), F32)),
        scratch_shapes=[in_buf] * 4 + [pltpu.SemaphoreType.DMA((4,))],
        compiler_params=params(),
        cost_estimate=cost(4 * slots * width * hidden, 10 << 20),
        name="expert_acts",
    )(home, recv_input, *own[:4], *far[:4])
    expert_rows = pl.pallas_call(
        back_kernel,
        grid=(slots // tile,),
        in_specs=[smem_spec, row_spec, act_spec, act_spec] + [any_spec] * 12,
        out_specs=row_spec,
        out_shape=sds((slots, width), BF16),
        scratch_shapes=[in_buf] * 4 + [out_buf] * 2 + [pltpu.SemaphoreType.DMA((6,))],
        compiler_params=params(),
        cost_estimate=cost(6 * slots * width * hidden, 14 << 20),
        name="expert_back",
    )(home, recv_grad, gate_act, up_act, *own, *far)
    returned = exchange(expert_rows)
    resid_grad = pl.pallas_call(
        combine_kernel,
        out_shape=sds((toks, width), BF16),
        compiler_params=params(),
        cost_estimate=cost(4 * slots * toks * width, 4 << 20),
        name="combine_rows",
    )(mix_hi, mix_lo, returned, out_grad)

    heads = skip_gain.shape[0]
    inner = out_proj.shape[0]
    seq_rows, state = b_proj.shape
    blocks = seq_rows // BLOCK
    flip = lambda i: blocks - 1 - i
    tok_in = pl.BlockSpec((BLOCK, inner), lambda i: (flip(i), 0))
    tok_st = pl.BlockSpec((BLOCK, state), lambda i: (flip(i), 0))
    blk_st = pl.BlockSpec((1, inner, state), lambda i: (flip(i), 0, 0))
    blk_w = pl.BlockSpec((1, heads, BLOCK, BLOCK), lambda i: (flip(i), 0, 0, 0))
    weights, to_start, to_end, x_end, block_sum, tail, total = pl.pallas_call(
        prepare_kernel,
        grid=(blocks,),
        in_specs=[pl.BlockSpec((heads, BLOCK), lambda i: (0, flip(i))), tok_st, tok_st, tok_in],
        out_specs=(blk_w, tok_in, tok_in, tok_in, blk_st, blk_st, whole((inner, state))),
        out_shape=(
            sds((blocks, heads, BLOCK, BLOCK), BF16),
            sds((seq_rows, inner), F32),
            sds((seq_rows, inner), F32),
            sds((seq_rows, inner), BF16),
            sds((blocks, inner, state), F32),
            sds((blocks, inner, state), F32),
            sds((inner, state), F32),
        ),
        compiler_params=params(),
        cost_estimate=cost(4e9, 16 << 20),
        name="scan_prepare",
    )(log_decay, b_proj, c_proj, ssd_x)

    rows_all = lax.all_gather(resid_grad, "head", axis=0, tiled=True)
    pay_rows = inner + 8
    ssd_grad, future, payload = pl.pallas_call(
        grad_kernel,
        grid=(blocks,),
        in_specs=[
            pl.BlockSpec((BLOCK, width), lambda i: (flip(i), 0)),
            whole((inner, width)),
            tok_st,
            tok_in,
            blk_st,
            whole((inner, state)),
        ],
        out_specs=(tok_in, blk_st, whole((pay_rows, state))),
        out_shape=(
            sds((seq_rows, inner), F32),
            sds((blocks, inner, state), F32),
            sds((pay_rows, state), F32),
        ),
        scratch_shapes=[pltpu.VMEM((inner, state), F32)],
        compiler_params=params(),
        cost_estimate=cost(2 * seq_rows * width * inner, 12 << 20),
        name="scan_grad",
    )(rows_all, out_proj, c_proj, to_start, block_sum, total)

    pays = [
        lax.ppermute(payload, "seq", [(s, s - d) for s in range(d, n_seq)]) for d in range(1, n_seq)
    ]
    skip_row = jnp.repeat(skip_gain, inner // heads).reshape(1, inner)
    part_x, part_b = pl.pallas_call(
        intra_kernel,
        grid=(blocks,),
        in_specs=[blk_w, tok_in, tok_in, tok_st, whole((1, inner))],
        out_specs=(tok_in, tok_st),
        out_shape=(sds((seq_rows, inner), F32), sds((seq_rows, state), F32)),
        compiler_params=params(),
        cost_estimate=cost(4e9, 12 << 20),
        name="scan_intra",
    )(weights, ssd_grad, ssd_x, c_proj, skip_row)
    partial_b, future_all = pl.pallas_call(
        cross_b_kernel,
        grid=(blocks,),
        in_specs=[whole((pay_rows, state))] * (n_seq - 1) + [blk_st, blk_st, tok_in, tok_st],
        out_specs=(tok_st, blk_st),
        out_shape=(sds((seq_rows, state), F32), sds((blocks, inner, state), BF16)),
        scratch_shapes=[pltpu.VMEM((inner, state), F32)],
        compiler_params=params(),
        cost_estimate=cost(4e8, 8 << 20),
        name="scan_cross_b",
    )(*pays, future, tail, x_end, part_b)
    shares = lax.all_to_all(
        partial_b.reshape(n_head, seq_rows // n_head, state), "head", split_axis=0, concat_axis=0, tiled=True
    )
    grad_x = pl.pallas_call(
        cross_x_kernel,
        grid=(blocks,),
        in_specs=[blk_st, tok_in, tok_st, tok_in],
        out_specs=tok_in,
        out_shape=sds((seq_rows, inner), F32),
        compiler_params=params(),
        cost_estimate=cost(4e8, 8 << 20),
        name="scan_cross_x",
    )(future_all, to_end, b_proj, part_x)
    b_grad = jnp.sum(shares, axis=0)
    return (resid_grad, grad_x, b_grad)


def solution(mesh):
    return jax.shard_map(
        shards,
        mesh=mesh,
        in_specs=(
            P(("seq", "head"), None),
            P(("seq", "head"), None),
            P(("seq", "head"), None),
            P(("seq", "head"), None),
            P(("seq", "head"), None, None),
            P(("seq", "head"), None, None),
            P(("seq", "head"), None, None),
            P("head", None),
            P("seq", "head"),
            P("seq", None),
            P("seq", None),
            P("head", "seq"),
            P("head"),
        ),
        out_specs=(P(("seq", "head"), None), P("seq", "head"), P(("seq", "head"), None)),
        check_vma=False,
    )
```

time: 665 us -> 341 us (0.51)
  waiting for transfers between devices: 323 us -> 126 us
  matrix products: 92.7 us -> 0 us
  Pallas kernels: 0 us -> 65.8 us
  blocking collectives: 115 us -> 50.5 us
  starting transfers between devices: 12.9 us -> 54.6 us
  local copies, waits for them, and re-layouts: 63.2 us -> 22 us
  other arithmetic: 36.2 us -> 1.91 us
    all_to_all x2 -> x3, waiting for transfers between devices: 230 us -> 44.9 us  [the longest x2 35.7 us: exchange(): lax.all_to_all(shaped, both, split_axis=0, concat_axis=0, tiled=True)]
    dot_general x12 -> x0, matrix products: 92.7 us -> none  [the longest x1 19.3 us: swiglu_back(): jnp.einsum('shcf,hdf->shcd', gate_grad, gate_w, preferred_element_type=jn...]
    pallas_call x0 -> x10, Pallas kernels: none -> 65.8 us  [the longest x1 13.7 us: shards(): pl.pallas_call(back_kernel, grid=(slots // tile,), in_specs=[smem_spec, r...]
    reduce_scatter x1 -> x0, waiting for transfers between devices: 59.6 us -> none  [shards(): lax.psum_scatter(partial_b, 'head', scatter_dimension=0, tiled=True)]
    ppermute x0 -> x16, waiting for transfers between devices: none -> 38.6 us  [the longest x3 38.3 us: shards(): y_halves = [lax.ppermute(a, both, over_y) for a in halves]]
    all_to_all x1, blocking collectives: 86.4 us -> 50.5 us  [exchange(): lax.all_to_all(shaped, both, split_axis=0, concat_axis=0, tiled=True)]
    ppermute x0 -> x16, starting transfers between devices: none -> 31.7 us  [the longest x3 12.2 us: shards(): far_own = [lax.ppermute(a, both, over_core) for a in halves]]
    gather x3 -> x0, local copies, waits for them, and re-layouts: 19.4 us -> none  [the longest x1 8.24 us: shards(): expert_rows[route_slot].reshape(tok_rows, top_count, feature_width)]
  transfers between devices with their start and end apart: 4 -> 20, of which waited for: 4 -> 7; matrix products, arithmetic and copies ran while one was open for 5% -> 1% of each run, Pallas kernels for 0% -> 10%
where the time goes in v1:
time: 341 us; the launch traced here: 335 us
  waiting for transfers between devices  126 us (37%)
  Pallas kernels  65.8 us (19%)
  starting transfers between devices  54.6 us (16%)
  blocking collectives  50.5 us (15%)
  local copies, waits for them, and re-layouts  22 us (6%)
  between operations  14.4 us (4%)
    all_to_all x1, blocking collectives, exchange(): lax.all_to_all(shaped, both, split_axis=0, concat_axis=0, tiled=True)  50.5 us
    all_gather x1, waiting for transfers between devices, shards(): rows_all = lax.all_gather(resid_grad, 'head', axis=0, tiled=True)  42.4 us
    ppermute x3, waiting for transfers between devices, shards(): y_halves = [lax.ppermute(a, both, over_y) for a in halves]  38.3 us
    all_to_all x2, waiting for transfers between devices, exchange(): lax.all_to_all(shaped, both, split_axis=0, concat_axis=0, tiled=True)  35.7 us
    unnamed x68, local copies, waits for them, and re-layouts  21.8 us
    all_to_all x2, starting transfers between devices, exchange(): lax.all_to_all(shaped, both, split_axis=0, concat_axis=0, tiled=True)  17.5 us
    pallas_call x1, Pallas kernels, shards(): pl.pallas_call(back_kernel, grid=(slots // tile,), in_specs=[smem_spec, r...  13.7 us
    ppermute x3, starting transfers between devices, shards(): far_own = [lax.ppermute(a, both, over_core) for a in halves]  12.2 us
  transfers between devices with their start and end apart: 20, of which 7 were waited for; matrix products, arithmetic and copies ran while one was open for 1% of the time, Pallas kernels for 10%

profile of v1, /device:TPU:0, one launch (start us, length us, event | category | flops | bytes accessed | tf_op | source)
XLA Modules:
  0.0 335.2 jit_solution(15932703234605412609)
XLA Ops:
  8.8 3.1 select_rows.1
  12.0 11.6 %all-to-all-start.1 = ((bf16[128,8,1536]{2,1,0:T(8,128)(2,1)}), bf16[128,8,1536]{2,1,0:T(8,128)(2,1)}, u32[]{:S(2)}, u32[]{:S(2)}) async-start(bf16[128,8,1536]{2,1,0:T(8,128)(2,1)} %bitcast.5), calls=%async_computation.1 | async-start | bytes 6291456 | tf_op jit(solution)/shard_map/all_to_all | solution.py:300
  23.6 2.9 select_grads.1
  28.0 35.7 %all-to-all-done.1 = bf16[128,8,1536]{2,1,0:T(8,128)(2,1)} async-done(((bf16[128,8,1536]{2,1,0:T(8,128)(2,1)}), bf16[128,8,1536]{2,1,0:T(8,128)(2,1)}, u32[]{:S(2)}, u32[]{:S(2)}) %all-to-all-start.1) | async-done | bytes 3145760 | tf_op jit(solution)/shard_map/all_to_all | solution.py:300
  63.7 5.9 %all-to-all-start = ((bf16[128,8,1536]{2,1,0:T(8,128)(2,1)}), bf16[128,8,1536]{2,1,0:T(8,128)(2,1)}, u32[]{:S(2)}, u32[]{:S(2)}) async-start(bf16[128,8,1536]{2,1,0:T(8,128)(2,1)} %bitcast.3), calls=%async_computation | async-start | bytes 6291456 | tf_op jit(solution)/shard_map/all_to_all | solution.py:300
  72.2 4.1 %collective-permute-start.2 = (bf16[1,1536,256]{2,1,0:T(8,128)(2,1)S(1)}, bf16[1,1536,256]{2,1,0:T(8,128)(2,1)S(1)}, u32[]{:S(2)}, u32[]{:S(2)}) collective-permute-start(bf16[1,1536,256]{2,1,0:T(8,128)(2,1)S(1)} %copy-done.4), channel_id=1, source_target_pairs={{0,16},{2,18},{4,20},{6,22},{8,24},{10,26},{12,28},{14,30},{17,1},... | collective-permute-start | bytes 2359304 | tf_op jit(solution)/shard_map/ppermute | solution.py:279
  77.7 5.9 %collective-permute-start.4 = (bf16[1,1536,256]{2,1,0:T(8,128)(2,1)S(1)}, bf16[1,1536,256]{2,1,0:T(8,128)(2,1)}, u32[]{:S(2)}, u32[]{:S(2)}) collective-permute-start(bf16[1,1536,256]{2,1,0:T(8,128)(2,1)S(1)} %copy-done.5), channel_id=1, source_target_pairs={{0,16},{2,18},{4,20},{6,22},{8,24},{10,26},{12,28},{14,30},{17,1},... | collective-permute-start | bytes 2359304 | tf_op jit(solution)/shard_map/ppermute | solution.py:279
  83.6 28.8 %collective-permute-done.refs_1_ = bf16[1,1536,256]{2,1,0:T(8,128)(2,1)S(1)} collective-permute-done((bf16[1,1536,256]{2,1,0:T(8,128)(2,1)S(1)}, bf16[1,1536,256]{2,1,0:T(8,128)(2,1)S(1)}, u32[]{:S(2)}, u32[]{:S(2)}) %collective-permute-start) | collective-permute-done | bytes 786464 | tf_op jit(solution)/shard_map/ppermute | solution.py:278
  112.4 2.2 collective-permute-start.3
  114.6 6.3 %collective-permute-done.1.refs_3_ = bf16[1,1536,256]{2,1,0:T(8,128)(2,1)} collective-permute-done((bf16[1,1536,256]{2,1,0:T(8,128)(2,1)S(1)}, bf16[1,1536,256]{2,1,0:T(8,128)(2,1)}, u32[]{:S(2)}, u32[]{:S(2)}) %collective-permute-start.1) | collective-permute-done | bytes 786464 | tf_op jit(solution)/shard_map/ppermute | solution.py:278
  121.0 2.2 collective-permute-start.5
  124.1 2.2 collective-permute-start.7
  126.2 3.2 collective-permute-done.6.refs_5_
  129.4 2.2 collective-permute-start.8
  132.7 8.0 %expert_acts.1 = (f32[1024,512]{1,0:T(8,128)}, f32[1024,512]{1,0:T(8,128)}) custom-call(s32[1]{0:T(128)} %bitcast.2.home_ref, bf16[1024,1536]{1,0:T(8,128)(2,1)} %bitcast.6.x_ref, bf16[1,1536,256]{2,1,0:T(8,128)(2,1)S(1)} %copy-done.4, bf16[1,1536,256]{2,1,0:T(8,128)(2,1)S(1)} %collective-permute-done.refs_1_, bf16[1,1536,256]{2,1,0:T(8,128)(2,1)S(1)} %copy-done.5, ...), custom_call_target="tpu_custom_call" | custom-call | flops 3221225472 | bytes 10485760 | tf_op jit(solution)/shard_map/expert_acts/pallas_call | solution.py:314
  141.9 13.7 %expert_back.1 = bf16[1024,1536]{1,0:T(8,128)(2,1)} custom-call(s32[1]{0:T(128)} %bitcast.2.home_ref, bf16[1024,1536]{1,0:T(8,128)(2,1)} %bitcast.4.g_ref, f32[1024,512]{1,0:T(8,128)} %get-tuple-element.29.gate_ref, f32[1024,512]{1,0:T(8,128)} %get-tuple-element.30.up_ref, bf16[1,1536,256]{2,1,0:T(8,128)(2,1)S(1)} %copy-done.4, ...), custom_call_target="tpu_custom_call" | custom-call | flops 4831838208 | bytes 14680064 | tf_op jit(solution)/shard_map/expert_back/pallas_call | solution.py:325
  155.6 50.5 %all_to_all.20 = bf16[128,8,1536]{2,1,0:T(8,128)(2,1)S(1)} all-to-all(bf16[128,8,1536]{2,1,0:T(8,128)(2,1)} %bitcast.14), channel_id=1, replica_groups=mesh['seq'=8,'head'=16] {'seq','head'}, dimensions={0} | all-to-all | bytes 6291456 | tf_op jit(solution)/shard_map/all_to_all | solution.py:300
  206.1 1.7 combine_rows.1
  207.8 3.0 copy.16.x_ref
  210.8 10.9 %scan_prepare.1 = (bf16[8,3,256,256]{3,2,1,0:T(8,128)(2,1)}, f32[2048,192]{1,0:T(8,128)}, f32[2048,192]{1,0:T(8,128)}, bf16[2048,192]{1,0:T(8,128)(2,1)S(1)}, f3...) custom-call(f32[3,2048]{1,0:T(4,128)S(1)} %copy-done.28, f32[2048,128]{1,0:T(8,128)S(1)} %copy-done.3, ...), custom_call_target="tpu_custom_call" | custom-call | flops 4000000000 | bytes 16777216 | tf_op jit(solution)/shard_map/scan_prepare/pallas_call | solution.py:354
  223.5 42.4 %all-gather.2.cloned.1.call-done.r_ref = bf16[2048,1536]{1,0:T(8,128)(2,1)} async-done(((bf16[128,1536]{1,0:T(8,128)(2,1)}), bf16[2048,1536]{1,0:T(8,128)(2,1)}) %all-gather.2.cloned.1.call-update) | async-done | bytes 6291472 | tf_op jit(solution)/shard_map/all_gather | solution.py:373
  268.1 8.9 %scan_grad.1 = (f32[2048,192]{1,0:T(8,128)S(1)}, f32[8,192,128]{2,1,0:T(8,128)S(1)}, f32[200,128]{1,0:T(8,128)S(1)}) custom-call(bf16[2048,1536]{1,0:T(8,128)(2,1)} %all-gather.2.cloned.1.call-done.r_ref, bf16[192,1536]{1,0:T(8,128)(2,1)S(1)} %copy-done.16, f32[2048,128]{1,0:T(8,128)S(1)} %copy-done.2, f32[2048,192]{1,0:T(8,128)} %get-tuple-element.31.ts_ref, ...), custom_call_target="tpu_custom_call" | custom-call | flops 1207959552 | bytes 12582912 | tf_op jit(solution)/shard_map/scan_grad/pallas_call | solution.py:375
  277.9 1.4 copy-done.26
  288.8 7.5 %scan_intra.1 = (f32[2048,192]{1,0:T(8,128)S(1)}, f32[2048,128]{1,0:T(8,128)S(1)}) custom-call(bf16[8,3,256,256]{3,2,1,0:T(8,128)(2,1)} %get-tuple-element.38.w_ref, f32[2048,192]{1,0:T(8,128)} %copy-done.26, f32[2048,192]{1,0:T(8,128)} %copy.16.x_ref, f32[2048,128]{1,0:T(8,128)S(1)} %copy-done.2, f32[1,192]{1,0:T(1,128)S(1)} %reshape_reshape.3.skip_ref), custom_call_target="tpu_custom_call" | custom-call | flops 4000000000 | bytes 12582912 | tf_op jit(solution)/shard_map/scan_intra/pallas_call | solution.py:402
  296.3 1.3 copy-done.1
  299.5 3.9 %scan_cross_b.1 = (f32[2048,128]{1,0:T(8,128)}, bf16[8,192,128]{2,1,0:T(8,128)(2,1)S(1)}) custom-call(f32[200,128]{1,0:T(8,128)S(1)} %collective-permute-done.9.refs_0_, f32[200,128]{1,0:T(8,128)S(1)} %copy-done.23, f32[200,128]{1,0:T(8,128)S(1)} %copy-done.25, f32[200,128]{1,0:T(8,128)S(1)} %collective-permute-done.12.refs_3_, ...), custom_call_target="tpu_custom_call" | custom-call | flops 400000000 | bytes 8388608 | tf_op jit(solution)/shard_map/scan_cross_b/pallas_call | solution.py:412
  303.4 5.3 %all-to-all-start.3 = ((f32[16,128,128]{2,1,0:T(8,128)}), f32[16,128,128]{2,1,0:T(8,128)}, u32[]{:S(2)}, u32[]{:S(2)}) async-start(f32[16,128,128]{2,1,0:T(8,128)} %bitcast.9), calls=%async_computation.3 | async-start | bytes 2097152 | tf_op jit(solution)/shard_map/all_to_all | solution.py:423
  308.8 1.6 copy-done
  310.3 5.2 %scan_cross_x.1 = f32[2048,192]{1,0:T(8,128)S(1)} custom-call(bf16[8,192,128]{2,1,0:T(8,128)(2,1)S(1)} %get-tuple-element.41.all_ref, f32[2048,192]{1,0:T(8,128)S(1)} %copy-done, f32[2048,128]{1,0:T(8,128)S(1)} %copy-done.3, f32[2048,192]{1,0:T(8,128)} %copy-done.1), custom_call_target="tpu_custom_call" | custom-call | flops 400000000 | bytes 8388608 | tf_op jit(solution)/shard_map/scan_cross_x/pallas_call | solution.py:426
  315.5 1.7 copy.18
  317.2 9.3 %all-to-all-done.3 = f32[16,128,128]{2,1,0:T(8,128)} async-done(((f32[16,128,128]{2,1,0:T(8,128)}), f32[16,128,128]{2,1,0:T(8,128)}, u32[]{:S(2)}, u32[]{:S(2)}) %all-to-all-start.3) | async-done | bytes 1048608 | tf_op jit(solution)/shard_map/all_to_all | solution.py:423
  326.5 1.9 reduce_sum.9
  (91 shorter events, 26.3 us)
Async XLA Ops:
  12.0 11.7 %copy-start.17 = (bf16[128,1536]{1,0:T(8,128)(2,1)S(1)}, bf16[128,1536]{1,0:T(8,128)(2,1)}, u32[]{:S(2)}) copy-start(bf16[128,1536]{1,0:T(8,128)(2,1)} %grad_ref.1) | copy-start | bytes 1179652
  12.0 11.7 %copy-start.30 = (s32[128,6]{0,1:T(8,128)S(1)}, s32[128,6]{0,1:T(8,128)}, u32[]{:S(2)}) copy-start(s32[128,6]{0,1:T(8,128)} %param.15) | copy-start | bytes 9220
  12.0 11.7 %copy-start.31 = (f32[128,6]{0,1:T(8,128)S(1)}, f32[128,6]{0,1:T(8,128)}, u32[]{:S(2)}) copy-start(f32[128,6]{0,1:T(8,128)} %param.16) | copy-start | bytes 9220
  12.0 51.7 %all-to-all-start.1 = ((bf16[128,8,1536]{2,1,0:T(8,128)(2,1)}), bf16[128,8,1536]{2,1,0:T(8,128)(2,1)}, u32[]{:S(2)}, u32[]{:S(2)}) async-start(bf16[128,8,1536]{2,1,0:T(8,128)(2,1)} %bitcast.5), calls=%async_computation.1 | async-start | bytes 6291456 | tf_op jit(solution)/shard_map/all_to_all | solution.py:300
  63.7 7.3 %copy-start.5 = (bf16[1,1536,256]{2,1,0:T(8,128)(2,1)S(1)}, bf16[1,1536,256]{2,1,0:T(8,128)(2,1)}, u32[]{:S(2)}) copy-start(bf16[1,1536,256]{2,1,0:T(8,128)(2,1)} %refs_2_.3) | copy-start | bytes 2359300
  63.7 12.7 %copy-start.6 = (bf16[1,256,1536]{2,1,0:T(8,128)(2,1)S(1)}, bf16[1,256,1536]{2,1,0:T(8,128)(2,1)}, u32[]{:S(2)}) copy-start(bf16[1,256,1536]{2,1,0:T(8,128)(2,1)} %refs_4_.1) | copy-start | bytes 2359300
  63.7 77.1 %all-to-all-start = ((bf16[128,8,1536]{2,1,0:T(8,128)(2,1)}), bf16[128,8,1536]{2,1,0:T(8,128)(2,1)}, u32[]{:S(2)}, u32[]{:S(2)}) async-start(bf16[128,8,1536]{2,1,0:T(8,128)(2,1)} %bitcast.3), calls=%async_computation | async-start | bytes 6291456 | tf_op jit(solution)/shard_map/all_to_all | solution.py:300
  69.6 196.3 %all-gather.2.cloned.1.call-start = ((), (), s32[]{:S(2)}) async-start(), calls=%async_computation.4 | async-start | bytes 6684672 | tf_op jit(solution)/shard_map/all_gather | solution.py:373
  69.6 42.8 %collective-permute-start = (bf16[1,1536,256]{2,1,0:T(8,128)(2,1)S(1)}, bf16[1,1536,256]{2,1,0:T(8,128)(2,1)S(1)}, u32[]{:S(2)}, u32[]{:S(2)}) collective-permute-start(bf16[1,1536,256]{2,1,0:T(8,128)(2,1)S(1)} %copy-done.4), channel_id=1, source_target_pairs={{1,0},{3,2},{5,4},{7,6},{9,8},{11,10},{13,12},{15,14},{16,17},{18,... | collective-permute-start | bytes 2359304 | tf_op jit(solution)/shard_map/ppermute | solution.py:278
  70.9 50.0 %collective-permute-start.1 = (bf16[1,1536,256]{2,1,0:T(8,128)(2,1)S(1)}, bf16[1,1536,256]{2,1,0:T(8,128)(2,1)}, u32[]{:S(2)}, u32[]{:S(2)}) collective-permute-start(bf16[1,1536,256]{2,1,0:T(8,128)(2,1)S(1)} %copy-done.5), channel_id=1, source_target_pairs={{1,0},{3,2},{5,4},{7,6},{9,8},{11,10},{13,12},{15,14},{16,17},{18,... | collective-permute-start | bytes 2359304 | tf_op jit(solution)/shard_map/ppermute | solution.py:278
  72.2 50.9 %collective-permute-start.2 = (bf16[1,1536,256]{2,1,0:T(8,128)(2,1)S(1)}, bf16[1,1536,256]{2,1,0:T(8,128)(2,1)S(1)}, u32[]{:S(2)}, u32[]{:S(2)}) collective-permute-start(bf16[1,1536,256]{2,1,0:T(8,128)(2,1)S(1)} %copy-done.4), channel_id=1, source_target_pairs={{0,16},{2,18},{4,20},{6,22},{8,24},{10,26},{12,28},{14,30},{17,1},... | collective-permute-start | bytes 2359304 | tf_op jit(solution)/shard_map/ppermute | solution.py:279
  76.4 53.0 %collective-permute-start.6 = (bf16[1,256,1536]{2,1,0:T(8,128)(2,1)S(1)}, bf16[1,256,1536]{2,1,0:T(8,128)(2,1)}, u32[]{:S(2)}, u32[]{:S(2)}) collective-permute-start(bf16[1,256,1536]{2,1,0:T(8,128)(2,1)S(1)} %copy-done.6), channel_id=1, source_target_pairs={{1,0},{3,2},{5,4},{7,6},{9,8},{11,10},{13,12},{15,14},{16,17},{18,... | collective-permute-start | bytes 2359304 | tf_op jit(solution)/shard_map/ppermute | solution.py:278
  77.7 53.9 %collective-permute-start.4 = (bf16[1,1536,256]{2,1,0:T(8,128)(2,1)S(1)}, bf16[1,1536,256]{2,1,0:T(8,128)(2,1)}, u32[]{:S(2)}, u32[]{:S(2)}) collective-permute-start(bf16[1,1536,256]{2,1,0:T(8,128)(2,1)S(1)} %copy-done.5), channel_id=1, source_target_pairs={{0,16},{2,18},{4,20},{6,22},{8,24},{10,26},{12,28},{14,30},{17,1},... | collective-permute-start | bytes 2359304 | tf_op jit(solution)/shard_map/ppermute | solution.py:279
  112.4 19.2 %collective-permute-start.3 = (bf16[1,1536,256]{2,1,0:T(8,128)(2,1)S(1)}, bf16[1,1536,256]{2,1,0:T(8,128)(2,1)}, u32[]{:S(2)}, u32[]{:S(2)}) collective-permute-start(bf16[1,1536,256]{2,1,0:T(8,128)(2,1)S(1)} %collective-permute-done.refs_1_), channel_id=1, source_target_pairs={{0,16},{2,18},{4,20},{6,22},{8,24},{10,26},{12,28},{14,30},{17,1},... | collective-permute-start | bytes 2359304 | tf_op jit(solution)/shard_map/ppermute | solution.py:280
  121.0 10.6 %collective-permute-start.5 = (bf16[1,1536,256]{2,1,0:T(8,128)(2,1)}, bf16[1,1536,256]{2,1,0:T(8,128)(2,1)}, u32[]{:S(2)}, u32[]{:S(2)}) collective-permute-start(bf16[1,1536,256]{2,1,0:T(8,128)(2,1)} %collective-permute-done.1.refs_3_), channel_id=1, source_target_pairs={{0,16},{2,18},{4,20},{6,22},{8,24},{10,26},{12,28},{14,30},{17,1},... | collective-permute-start | bytes 2359304 | tf_op jit(solution)/shard_map/ppermute | solution.py:280
  124.1 16.7 %collective-permute-start.7 = (bf16[1,256,1536]{2,1,0:T(8,128)(2,1)S(1)}, bf16[1,256,1536]{2,1,0:T(8,128)(2,1)}, u32[]{:S(2)}, u32[]{:S(2)}) collective-permute-start(bf16[1,256,1536]{2,1,0:T(8,128)(2,1)S(1)} %copy-done.6), channel_id=1, source_target_pairs={{0,16},{2,18},{4,20},{6,22},{8,24},{10,26},{12,28},{14,30},{17,1},... | collective-permute-start | bytes 2359304 | tf_op jit(solution)/shard_map/ppermute | solution.py:279
  129.4 11.3 %collective-permute-start.8 = (bf16[1,256,1536]{2,1,0:T(8,128)(2,1)}, bf16[1,256,1536]{2,1,0:T(8,128)(2,1)}, u32[]{:S(2)}, u32[]{:S(2)}) collective-permute-start(bf16[1,256,1536]{2,1,0:T(8,128)(2,1)} %collective-permute-done.6.refs_5_), channel_id=1, source_target_pairs={{0,16},{2,18},{4,20},{6,22},{8,24},{10,26},{12,28},{14,30},{17,1},... | collective-permute-start | bytes 2359304 | tf_op jit(solution)/shard_map/ppermute | solution.py:280
  155.6 50.5 %copy-start.19 = (bf16[128,1024]{1,0:T(8,128)(2,1)S(1)}, bf16[128,1024]{1,0:T(8,128)(2,1)}, u32[]{:S(2)}) copy-start(bf16[128,1024]{1,0:T(8,128)(2,1)} %copy-done.18) | copy-start | bytes 786436
  155.6 50.5 %copy-start.21 = (bf16[128,1024]{1,0:T(8,128)(2,1)S(1)}, bf16[128,1024]{1,0:T(8,128)(2,1)}, u32[]{:S(2)}) copy-start(bf16[128,1024]{1,0:T(8,128)(2,1)} %copy-done.20) | copy-start | bytes 786436
  268.1 13.7 %copy-start.32 = (f32[3]{0:T(128)S(1)}, f32[3]{0:T(128)}, u32[]{:S(2)}) copy-start(f32[3]{0:T(128)} %param.25) | copy-start | bytes 40
  279.2 6.9 %collective-permute-start.10 = (f32[200,128]{1,0:T(8,128)S(1)}, f32[200,128]{1,0:T(8,128)S(1)}, u32[]{:S(2)}, u32[]{:S(2)}) collective-permute-start(f32[200,128]{1,0:T(8,128)S(1)} %get-tuple-element.34), channel_id=1, source_target_pairs={{32,0},{48,16},{64,32},{80,48},{96,64},{112,80},{33,1},{49,17},{65... | collective-permute-start | bytes 307208 | tf_op jit(solution)/shard_map/ppermute | solution.py:399
  280.5 6.9 %collective-permute-start.11 = (f32[200,128]{1,0:T(8,128)S(1)}, f32[200,128]{1,0:T(8,128)S(1)}, u32[]{:S(2)}, u32[]{:S(2)}) collective-permute-start(f32[200,128]{1,0:T(8,128)S(1)} %get-tuple-element.34), channel_id=1, source_target_pairs={{48,0},{64,16},{80,32},{96,48},{112,64},{49,1},{65,17},{81,33},{97... | collective-permute-start | bytes 307208 | tf_op jit(solution)/shard_map/ppermute | solution.py:399
  282.0 15.7 %collective-permute-start.12 = (f32[200,128]{1,0:T(8,128)S(1)}, f32[200,128]{1,0:T(8,128)S(1)}, u32[]{:S(2)}, u32[]{:S(2)}) collective-permute-start(f32[200,128]{1,0:T(8,128)S(1)} %get-tuple-element.34), channel_id=1, source_target_pairs={{64,0},{80,16},{96,32},{112,48},{65,1},{81,17},{97,33},{113,49},{6... | collective-permute-start | bytes 307208 | tf_op jit(solution)/shard_map/ppermute | solution.py:399
  283.3 14.4 %collective-permute-start.13 = (f32[200,128]{1,0:T(8,128)S(1)}, f32[200,128]{1,0:T(8,128)S(1)}, u32[]{:S(2)}, u32[]{:S(2)}) collective-permute-start(f32[200,128]{1,0:T(8,128)S(1)} %get-tuple-element.34), channel_id=1, source_target_pairs={{80,0},{96,16},{112,32},{81,1},{97,17},{113,33},{82,2},{98,18},{11... | collective-permute-start | bytes 307208 | tf_op jit(solution)/shard_map/ppermute | solution.py:399
  284.6 13.1 %collective-permute-start.14 = (f32[200,128]{1,0:T(8,128)S(1)}, f32[200,128]{1,0:T(8,128)S(1)}, u32[]{:S(2)}, u32[]{:S(2)}) collective-permute-start(f32[200,128]{1,0:T(8,128)S(1)} %get-tuple-element.34), channel_id=1, source_target_pairs={{96,0},{112,16},{97,1},{113,17},{98,2},{114,18},{99,3},{115,19},{1... | collective-permute-start | bytes 307208 | tf_op jit(solution)/shard_map/ppermute | solution.py:399
  286.1 10.2 %copy-start.22 = (f32[200,128]{1,0:T(8,128)}, f32[200,128]{1,0:T(8,128)S(1)}, u32[]{:S(2)}) copy-start(f32[200,128]{1,0:T(8,128)S(1)} %collective-permute-done.10.refs_1_) | copy-start | bytes 307204
  286.1 11.5 %collective-permute-start.15 = (f32[200,128]{1,0:T(8,128)S(1)}, f32[200,128]{1,0:T(8,128)S(1)}, u32[]{:S(2)}, u32[]{:S(2)}) collective-permute-start(f32[200,128]{1,0:T(8,128)S(1)} %get-tuple-element.34), channel_id=1, source_target_pairs={{112,0},{113,1},{114,2},{115,3},{116,4},{117,5},{118,6},{119,7},{1... | collective-permute-start | bytes 307208 | tf_op jit(solution)/shard_map/ppermute | solution.py:399
  287.4 8.9 %copy-start.24 = (f32[200,128]{1,0:T(8,128)}, f32[200,128]{1,0:T(8,128)S(1)}, u32[]{:S(2)}) copy-start(f32[200,128]{1,0:T(8,128)S(1)} %collective-permute-done.11.refs_2_) | copy-start | bytes 307204
  287.4 10.2 %collective-permute-start.9 = (f32[200,128]{1,0:T(8,128)S(1)}, f32[200,128]{1,0:T(8,128)S(1)}, u32[]{:S(2)}, u32[]{:S(2)}) collective-permute-start(f32[200,128]{1,0:T(8,128)S(1)} %get-tuple-element.34), channel_id=1, source_target_pairs={{16,0},{32,16},{48,32},{64,48},{80,64},{96,80},{112,96},{17,1},{33... | collective-permute-start | bytes 307208 | tf_op jit(solution)/shard_map/ppermute | solution.py:399
  288.7 9.0 %copy-start.11 = (f32[8,192,128]{2,1,0:T(8,128)S(1)}, f32[8,192,128]{2,1,0:T(8,128)}, u32[]{:S(2)}) copy-start(f32[8,192,128]{2,1,0:T(8,128)} %copy-done.10) | copy-start | bytes 2359300
  288.7 9.0 %copy-start.13 = (f32[8,192,128]{2,1,0:T(8,128)S(1)}, f32[8,192,128]{2,1,0:T(8,128)}, u32[]{:S(2)}) copy-start(f32[8,192,128]{2,1,0:T(8,128)} %copy-done.12) | copy-start | bytes 2359300
  303.4 23.1 %all-to-all-start.3 = ((f32[16,128,128]{2,1,0:T(8,128)}), f32[16,128,128]{2,1,0:T(8,128)}, u32[]{:S(2)}, u32[]{:S(2)}) async-start(f32[16,128,128]{2,1,0:T(8,128)} %bitcast.9), calls=%async_computation.3 | async-start | bytes 2097152 | tf_op jit(solution)/shard_map/all_to_all | solution.py:423
  (21 other events, 32.2 us)
Sparse Core Ops, SparseCore 0:
  208.0 57.8 all-gather.1
